TPU v7x, 32 devices: a whole 2x2x4 slice. The times are simulated.
32 devices in a mesh: dp: 4 (over x, core), seq: 8 (over z, y).
Axes of the slice: x: 2, y: 2, z: 4, core: 2. Of those that a mesh axis runs over, the one named last changes fastest.
Arguments:
- tokens: bfloat16 [32768, 1152], P(('dp', 'seq')), may hold values from -6 to 6
- condition: bfloat16 [128, 1152], P('dp'), may hold values from -6 to 6
- lengths: int32 [128], P(('dp', 'seq')), may hold values from 1 to 256, 22937 in all
- kept_index: int32 [128, 256], P(('dp', 'seq')), may hold values from 0 to 255, each once within a row
- heads_weight: bfloat16 [1152, 3456], P('seq'), may hold values from -0.1875 to 0.1875
- heads_bias: bfloat16 [2304], replicated, may hold values from -1.5 to 1.5
- merge_weight: bfloat16 [1152, 1152], P('seq'), may hold values from -1.5 to 1.5
- merge_bias: bfloat16 [1152], replicated, may hold values from -4 to 4
- up_weight: bfloat16 [1152, 4608], P('seq'), may hold values from -0.1875 to 0.1875
- up_bias: bfloat16 [4608], replicated, may hold values from -4 to 4
- down_weight: bfloat16 [1152, 4608], P('seq'), may hold values from -0.1875 to 0.1875
- down_bias: bfloat16 [1152], replicated, may hold values from -4 to 4
- modulate_weight: bfloat16 [1152, 6912], P('seq'), may hold values from -0.1875 to 0.1875
- modulate_bias: bfloat16 [6912], replicated, may hold values from -4 to 4
- relative_table: bfloat16 [16, 961], replicated, may hold values from -6 to 6
- cotangent: bfloat16 [32768, 1152], P(('dp', 'seq')), may hold values from -6 to 6
Outputs:
- output: bfloat16 [32768, 1152], P(('dp', 'seq'))
- tokens_grad: float32 [32768, 1152], P(('dp', 'seq'))
- heads_weight_grad: float32 [1152, 3456], P('seq')
- merge_weight_grad: float32 [1152, 1152], P('seq')
- up_weight_grad: float32 [1152, 4608], P('seq')
- down_weight_grad: float32 [1152, 4608], P('seq')
- modulate_weight_grad: float32 [1152, 6912], P('seq')
- heads_bias_grad: float32 [2304], replicated
- merge_bias_grad: float32 [1152], replicated
- up_bias_grad: float32 [4608], replicated
- down_bias_grad: float32 [1152], replicated
- modulate_bias_grad: float32 [6912], replicated
- relative_table_grad: float32 [16, 961], replicated
Inputs may be any that keep to these rules, and one draw needn't show every extreme that they name: The first lengths[s] slots of sample s hold its kept tokens, the rest are empty. Each sample's row is a permutation of the 256 patch positions; slot r's patch lies at row kept_index // 16, column kept_index % 16.
All inputs are finite; a program needn't handle non-finite values. No bound on the sum of `lengths` on one device may be relied on, other than what follows from the above.
Results may differ from a plain program's by a relative error of at most 0.019.
Values may be sent and summed in bfloat16 or wider, within the bound.
No kernel may reach another device: no remote copies, remote signals or barrier semaphores. Data moves between devices by JAX's collectives and lax.ppermute only.
A program may use at most 320 MiB of HBM per device.

v0:
```python
from functools import partial
import math
import jax
import jax.numpy as jnp
from jax import lax
from jax.sharding import PartitionSpec as P

D = 1152
HEADS = 16
HEAD = 72
FF = 4608
SIDE = 16
MICRO = 2
SAMP_DEV = 4
GRID = 256
epsilon = 1e-06


def layer_norm(values):
    center = values - jnp.mean(values, axis=-1, keepdims=True)
    spread = jnp.mean(center * center, axis=-1, keepdims=True)
    return center * lax.rsqrt(spread + epsilon)


def modulated(values, scales, shifts):
    return layer_norm(values) * (1.0 + scales) + shifts


def gelu_tanh(values):
    return jax.nn.gelu(values, approximate=True)


def fold_rows(left, portion):
    return jnp.dot(left, portion, preferred_element_type=jnp.float32)


def right_transposed(left, portion):
    return lax.dot_general(
        left, portion, (((1,), (1,)), ((), ())), preferred_element_type=jnp.float32
    )


def column_outer(left, right):
    return lax.dot_general(
        left, right, (((0,), (0,)), ((), ())), preferred_element_type=jnp.float32
    )


def relative_index(positions):
    row_place = positions // SIDE
    col_place = positions % SIDE
    row_gap = row_place[..., :, None] - row_place[..., None, :] + (SIDE - 1)
    col_gap = col_place[..., :, None] - col_place[..., None, :] + (SIDE - 1)
    return row_gap * (2 * SIDE - 1) + col_gap


def slot_onehot(index_pair):
    return (index_pair[..., :, None] == jnp.arange(GRID)[None, None, :]).astype(jnp.bfloat16)


def pair_scores(packed, lens_pair, index_pair, position_bias):
    parts = packed.reshape(2, GRID, 3, HEADS, HEAD)
    queries = parts[:, :, 0]
    key_part = parts[:, :, 1]
    value_part = parts[:, :, 2]
    scaling = 1.0 / math.sqrt(HEAD)
    onehot = slot_onehot(index_pair)
    rows_placed = jnp.einsum(
        "srp,hpq->hsrq", onehot, position_bias, preferred_element_type=jnp.float32
    ).astype(jnp.bfloat16)
    bias_pair = jnp.einsum(
        "hsrq,skq->hsrk", rows_placed, onehot, preferred_element_type=jnp.float32
    )
    scores = (
        jnp.einsum("sqhe,skhe->hsqk", queries, key_part, preferred_element_type=jnp.float32)
        * scaling
    )
    scores = scores + bias_pair
    living = jnp.arange(GRID)[None, :] < lens_pair[:, None]
    scores = jnp.where(living[None, :, None, :], scores, -1e30)
    return (scores, queries, key_part, value_part, onehot)


def attend_pair(arguments, position_bias):
    packed, lens_pair, index_pair = arguments
    scores, queries, key_part, value_part, onehot = pair_scores(
        packed, lens_pair, index_pair, position_bias
    )
    peak = jnp.max(scores, axis=-1, keepdims=True)
    expo = jnp.exp(scores - peak)
    mass = jnp.sum(expo, axis=-1, keepdims=True)
    probs_low = (expo / mass).astype(jnp.bfloat16)
    mixed = jnp.einsum("hsqk,skhe->sqhe", probs_low, value_part, preferred_element_type=jnp.float32)
    return (mixed.astype(jnp.bfloat16).reshape(2 * GRID, D), (peak + jnp.log(mass))[..., 0])


def attend_pair_back(arguments, position_bias):
    packed, lens_pair, index_pair, logsum, grad_mixed = arguments
    scores, queries, key_part, value_part, onehot = pair_scores(
        packed, lens_pair, index_pair, position_bias
    )
    probs = jnp.exp(scores - logsum[..., None])
    grad_mixed = grad_mixed.reshape(2, GRID, HEADS, HEAD)
    grad_probs = jnp.einsum(
        "sqhe,skhe->hsqk", grad_mixed, value_part, preferred_element_type=jnp.float32
    )
    inner = jnp.sum(probs * grad_probs, axis=-1, keepdims=True)
    grad_scores = (probs * (grad_probs - inner)).astype(jnp.bfloat16)
    scaling = 1.0 / math.sqrt(HEAD)
    grad_query = (
        jnp.einsum("hsqk,skhe->sqhe", grad_scores, key_part, preferred_element_type=jnp.float32)
        * scaling
    )
    grad_key = (
        jnp.einsum("hsqk,sqhe->skhe", grad_scores, queries, preferred_element_type=jnp.float32)
        * scaling
    )
    grad_value = jnp.einsum(
        "hsqk,sqhe->skhe",
        probs.astype(jnp.bfloat16),
        grad_mixed,
        preferred_element_type=jnp.float32,
    )
    stacked = (
        jnp.stack([grad_query, grad_key, grad_value], axis=2)
        .astype(jnp.bfloat16)
        .reshape(2 * GRID, 3 * D)
    )
    rows_back = jnp.einsum(
        "hsrk,srp->hspk", grad_scores, onehot, preferred_element_type=jnp.float32
    ).astype(jnp.bfloat16)
    placed_grad = jnp.einsum("hspk,skq->hpq", rows_back, onehot, preferred_element_type=jnp.float32)
    return (stacked, placed_grad)


def offsets_table(placed_grad):
    spots = jnp.arange(SIDE)
    reach = jnp.arange(2 * SIDE - 1)
    gaps = (
        spots[:, None, None] - spots[None, :, None] + (SIDE - 1) == reach[None, None, :]
    ).astype(jnp.float32)
    grid_grad = placed_grad.reshape(HEADS, SIDE, SIDE, SIDE, SIDE)
    by_rows = jnp.einsum("hwxyz,wya->haxz", grid_grad, gaps, precision=lax.Precision.HIGHEST)
    return jnp.einsum("haxz,xzb->hab", by_rows, gaps, precision=lax.Precision.HIGHEST).reshape(
        HEADS, (2 * SIDE - 1) ** 2
    )


def local(
    tokens,
    condition,
    lengths,
    kept_index,
    heads_weight,
    heads_bias,
    merge_weight,
    merge_bias,
    up_weight,
    up_bias,
    down_weight,
    down_bias,
    modulate_weight,
    modulate_bias,
    relative_table,
    cotangent,
):
    position = lax.axis_index("seq")
    position_bias = jnp.take(relative_table, relative_index(jnp.arange(GRID)), axis=1)
    own_cond = lax.dynamic_slice_in_dim(condition, position * SAMP_DEV, SAMP_DEV, 0)
    own_silu = jax.nn.silu(own_cond.astype(jnp.float32)).astype(jnp.bfloat16)
    modulation = fold_rows(own_silu, lax.all_gather(modulate_weight, "seq", axis=0, tiled=True))
    modulation = (modulation + modulate_bias.astype(jnp.float32)).reshape(SAMP_DEV, 1, 6, D)
    full_bias = jnp.concatenate(
        [heads_bias[:D], jnp.zeros((D,), jnp.bfloat16), heads_bias[D:]]
    ).astype(jnp.float32)
    parts_count = MICRO
    samples = SAMP_DEV // parts_count
    rows = samples * GRID
    pairs = samples // 2
    kept = {
        "out": [],
        "tgrad": [],
        "mgrad": [],
        "hone": [],
        "gpack": [],
        "attn": [],
        "gbranch": [],
        "htwo": [],
        "gup": [],
        "gmlp": [],
        "act": [],
    }
    placed_total = jnp.zeros((HEADS, GRID, GRID), jnp.float32)
    for part in range(parts_count):
        slab = tokens[part * rows : (part + 1) * rows].astype(jnp.float32).reshape(samples, GRID, D)
        mods = modulation[part * samples : (part + 1) * samples]
        shift_one, scale_one, gate_one, shift_two, scale_two, gate_two = [
            mods[:, :, index] for index in range(6)
        ]
        lens_part = lengths[part * samples : (part + 1) * samples]
        index_part = kept_index[part * samples : (part + 1) * samples]
        living = (jnp.arange(GRID)[None, :] < lens_part[:, None])[:, :, None]
        hidden_one = modulated(slab, scale_one, shift_one).astype(jnp.bfloat16).reshape(rows, D)
        packed = (
            fold_rows(hidden_one, lax.all_gather(heads_weight, "seq", axis=0, tiled=True))
            + full_bias
        ).astype(jnp.bfloat16)
        packed_pairs = packed.reshape(pairs, 2 * GRID, 3 * D)
        lens_pairs = lens_part.reshape(pairs, 2)
        index_pairs = index_part.reshape(pairs, 2, GRID)
        attended, logsum = lax.map(
            partial(attend_pair, position_bias=position_bias),
            (packed_pairs, lens_pairs, index_pairs),
        )
        attended = attended.reshape(rows, D)
        branch = fold_rows(
            attended, lax.all_gather(merge_weight, "seq", axis=0, tiled=True)
        ) + merge_bias.astype(jnp.float32)
        branch = branch.reshape(samples, GRID, D)
        middle = slab + gate_one * branch
        hidden_two = modulated(middle, scale_two, shift_two).astype(jnp.bfloat16).reshape(rows, D)
        up_value = fold_rows(
            hidden_two, lax.all_gather(up_weight, "seq", axis=0, tiled=True)
        ) + up_bias.astype(jnp.float32)
        activated = gelu_tanh(up_value).astype(jnp.bfloat16)
        mlp_out = right_transposed(
            activated, lax.all_gather(down_weight, "seq", axis=0, tiled=True)
        )
        mlp_out = (mlp_out + down_bias.astype(jnp.float32)).reshape(samples, GRID, D)
        final = jnp.where(living, middle + gate_two * mlp_out, 0.0)
        kept["out"].append(final.astype(jnp.bfloat16).reshape(rows, D))
        grad_final = jnp.where(
            living,
            cotangent[part * rows : (part + 1) * rows]
            .astype(jnp.float32)
            .reshape(samples, GRID, D),
            0.0,
        )
        gate_two_grad = jnp.sum(grad_final * mlp_out, axis=1, keepdims=True)
        grad_mlp = (gate_two * grad_final).astype(jnp.bfloat16).reshape(rows, D)
        grad_act = fold_rows(grad_mlp, lax.all_gather(down_weight, "seq", axis=0, tiled=True))
        grad_up = jax.vjp(gelu_tanh, up_value)[1](grad_act)[0].astype(jnp.bfloat16)
        grad_hidden_two = right_transposed(
            grad_up, lax.all_gather(up_weight, "seq", axis=0, tiled=True)
        )
        middle_ln, scale_two_grad, shift_two_grad = jax.vjp(
            modulated, middle, scale_two, shift_two
        )[1](grad_hidden_two.reshape(samples, GRID, D))
        grad_middle = grad_final + middle_ln
        gate_one_grad = jnp.sum(grad_middle * branch, axis=1, keepdims=True)
        grad_branch = (gate_one * grad_middle).astype(jnp.bfloat16).reshape(rows, D)
        grad_attended = right_transposed(
            grad_branch, lax.all_gather(merge_weight, "seq", axis=0, tiled=True)
        ).astype(jnp.bfloat16)
        grad_packed, placed_parts = lax.map(
            partial(attend_pair_back, position_bias=position_bias),
            (
                packed_pairs,
                lens_pairs,
                index_pairs,
                logsum,
                grad_attended.reshape(pairs, 2 * GRID, D),
            ),
        )
        grad_packed = grad_packed.reshape(rows, 3 * D)
        placed_total = placed_total + jnp.sum(placed_parts, axis=0)
        grad_hidden_one = right_transposed(
            grad_packed, lax.all_gather(heads_weight, "seq", axis=0, tiled=True)
        )
        slab_ln, scale_one_grad, shift_one_grad = jax.vjp(modulated, slab, scale_one, shift_one)[1](
            grad_hidden_one.reshape(samples, GRID, D)
        )
        kept["tgrad"].append((grad_middle + slab_ln).reshape(rows, D))
        kept["mgrad"].append(
            jnp.concatenate(
                [
                    shift_one_grad,
                    scale_one_grad,
                    gate_one_grad,
                    shift_two_grad,
                    scale_two_grad,
                    gate_two_grad,
                ],
                axis=-1,
            ).reshape(samples, 6 * D)
        )
        kept["hone"].append(hidden_one)
        kept["gpack"].append(grad_packed)
        kept["attn"].append(attended)
        kept["gbranch"].append(grad_branch)
        kept["htwo"].append(hidden_two)
        kept["gup"].append(grad_up)
        kept["gmlp"].append(grad_mlp)
        kept["act"].append(activated)
    table_grad = offsets_table(placed_total)
    joined = {name: jnp.concatenate(items, axis=0) for name, items in kept.items()}
    mod_grad = joined["mgrad"].astype(jnp.bfloat16)
    pieces = [
        column_outer(joined["hone"], joined["gpack"]),
        column_outer(joined["attn"], joined["gbranch"]),
        column_outer(joined["htwo"], joined["gup"]),
        column_outer(joined["gmlp"], joined["act"]),
        column_outer(own_silu, mod_grad),
    ]
    summed = lax.psum_scatter(
        jnp.concatenate(pieces, axis=1).astype(jnp.bfloat16), "seq", scatter_dimension=0, tiled=True
    )
    share = lax.psum_scatter(summed, "dp", scatter_dimension=0, tiled=True).astype(jnp.float32)
    replicated = lax.all_gather(share.astype(jnp.bfloat16), "dp", axis=0, tiled=True).astype(
        share.dtype
    )
    packed_sums = jnp.sum(joined["gpack"], axis=0, dtype=jnp.float32)
    heads_part = jnp.concatenate([packed_sums[:D], packed_sums[2 * D :]])
    merge_part = jnp.sum(joined["gbranch"], axis=0, dtype=jnp.float32)
    up_part = jnp.sum(joined["gup"], axis=0, dtype=jnp.float32)
    down_part = jnp.sum(joined["gmlp"], axis=0, dtype=jnp.float32)
    modulate_part = jnp.sum(mod_grad, axis=0, dtype=jnp.float32)
    heads_total, merge_total, up_total, down_total, modulate_total, table_total = lax.psum(
        (heads_part, merge_part, up_part, down_part, modulate_part, table_grad), ("dp", "seq")
    )
    edges = [0, 3 * D, 4 * D, 4 * D + FF, 4 * D + 2 * FF, 10 * D + 2 * FF]
    return (
        joined["out"],
        joined["tgrad"],
        replicated[:, edges[0] : edges[1]],
        replicated[:, edges[1] : edges[2]],
        replicated[:, edges[2] : edges[3]],
        replicated[:, edges[3] : edges[4]],
        replicated[:, edges[4] : edges[5]],
        heads_total,
        merge_total,
        up_total,
        down_total,
        modulate_total,
        table_total,
    )


def solution(mesh):
    in_specs = (
        P(("dp", "seq"), None),
        P("dp", None),
        P(("dp", "seq")),
        P(("dp", "seq"), None),
        P("seq", None),
        P(),
        P("seq", None),
        P(),
        P("seq", None),
        P(),
        P("seq", None),
        P(),
        P("seq", None),
        P(),
        P(),
        P(("dp", "seq"), None),
    )
    out_specs = (
        P(("dp", "seq"), None),
        P(("dp", "seq"), None),
        P("seq", None),
        P("seq", None),
        P("seq", None),
        P("seq", None),
        P("seq", None),
        P(),
        P(),
        P(),
        P(),
        P(),
        P(),
    )
    return jax.shard_map(local, mesh=mesh, in_specs=in_specs, out_specs=out_specs, check_vma=False)
```

profile of v0, /device:TPU:8, one launch (start us, length us, event | category | flops | bytes accessed | tf_op | source)
XLA Modules:
  0.0 2067.6 jit_solution(3447131822799105786)
XLA Ops:
  26.2 227.7 %gather_fusion = bf16[65536,16]{1,0:T(8,128)(2,1)} fusion(bf16[16,961]{0,1:T(8,128)(2,1)S(1)} %copy.147, s32[65536]{0:T(1024)S(1)} %broadcast_clamp_fusion), kind=kCustom, calls=%fused_computation | custom fusion | bytes 4456448 | tf_op jit(solution)/shard_map/jit(_take)/gather | solution.py:168
  253.8 16.7 copy.148
  292.3 54.5 %all-gather.10.cloned.1.call-done = bf16[1152,3456]{1,0:T(8,128)(2,1)} async-done(((bf16[144,3456]{1,0:T(8,128)(2,1)}), bf16[1152,3456]{1,0:T(8,128)(2,1)}) %all-gather.10.cloned.1.call-update) | async-done | bytes 7962640 | tf_op jit(solution)/shard_map/all_gather | solution.py:205
  346.7 9.5 add_convert_fusion.1
  362.1 8.3 reshape.859
  370.4 15.9 fusion.217
  411.4 11.2 add_convert_fusion
  428.3 8.3 reshape.861
  467.8 87.5 %all-gather.14.cloned.1.call-done = bf16[1152,4608]{1,0:T(8,128)(2,1)} async-done(((bf16[144,4608]{1,0:T(8,128)(2,1)}), bf16[1152,4608]{1,0:T(8,128)(2,1)}) %all-gather.14.cloned.1.call-update) | async-done | bytes 10616848 | tf_op jit(solution)/shard_map/all_gather | solution.py:223
  555.3 11.7 fusion.231
  566.9 8.9 fusion.230
  575.8 132.2 %all-gather.16.cloned.1.call-done = bf16[1152,4608]{1,0:T(8,128)(2,1)} async-done(((bf16[144,4608]{1,0:T(8,128)(2,1)}), bf16[1152,4608]{1,0:T(8,128)(2,1)}) %all-gather.16.cloned.1.call-update) | async-done | bytes 10616848 | tf_op jit(solution)/shard_map/all_gather | solution.py:227
  708.0 11.6 fusion.232
  719.6 24.2 %fusion.11 = (bf16[512,4608]{1,0:T(8,128)(2,1)}, bf16[512,4608]{1,0:T(8,128)(2,1)}, bf16[512,4608]{1,0:T(8,128)(2,1)}, bf16[512,4608]{1,0:T(8,128)(2,1)}) fusion(f32[512,4608]{1,0:T(8,128)} %fusion.230, f32[4608]{0:T(1024)S(1)} %copy-done.104, f32[512,4608]{1,0:T(8,128)} %fusion.231, f32[512,4608]{1,0:T(8,128)} %fusion.232, ...), kind=kOutput, calls=%fused_computation.21 | convolution fusion | flops 5544345600 | bytes 59000832 | tf_op jit(solution)/shard_map/dot_general | solution.py:34
  743.8 12.7 multiply_reduce_fusion.11
  757.2 13.2 multiply_reduce_fusion.9
  771.0 14.4 fusion.210
  785.5 13.1 fusion.211
  883.6 8.8 multiply_reduce_fusion.10
  899.8 10.3 multiply_reduce_fusion.8
  916.6 10.9 fusion.4
  931.0 17.3 fusion.3
  948.4 16.6 fusion.2
  975.5 8.7 fusion.1
  984.2 748.7 %reduce-scatter.4.cloned.1.call-done = bf16[144,20736]{1,0:T(8,128)(2,1)} async-done(((bf16[1152,20736]{1,0:T(8,128)(2,1)}), bf16[144,20736]{1,0:T(8,128)(2,1)}) %reduce-scatter.4.cloned.1.call-update) | async-done | bytes 5971984 | tf_op jit(solution)/shard_map/reduce_scatter | solution.py:305
  1732.9 62.0 %fusion = bf16[40,20736]{1,0:T(8,128)(2,1)} fusion(bf16[144,20736]{1,0:T(8,128)(2,1)} %reduce-scatter.4.cloned.1.call-done), kind=kCustom, calls=%all-reduce-scatter | all-reduce-scatter fusion | flops 3317761 | bytes 7631360
  1800.4 17.0 concatenate.72
  1827.4 8.1 bitcast_add_fusion.2
  1835.4 19.8 add.547
  1855.2 33.3 %fusion.185 = f32[31,16,16,16,1]{0,3,2,4,1:T(8,128)} fusion(f32[16,16,16,16,16]{4,3,2,1,0:T(8,128)} %add.547, s32[16,16]{1,0:T(8,128)S(1)} %subtract_add_fusion), kind=kOutput, calls=%fused_computation.258 | convolution fusion | flops 390078208 | bytes 4703232 | tf_op jit(solution)/shard_map/hwxyz,wya->haxz/dot_general | solution.py:143
  1916.3 10.3 reshape.899
  1938.7 113.8 %all-reduce.5.cloned.1.call-done = (f32[2304]{0:T(1024)}, f32[1152]{0:T(1024)}, f32[4608]{0:T(1024)}, f32[1152]{0:T(1024)}, f32[6912]{0:T(1024)}, /*index=5*/f32[16,961]{1,0:T(8,128)}) async-done(((f32[2304]{0:T(1024)}, f32[1152]{0:T(1024)}, f32[4608]{0:T(1024)}, f32[1152]{0:T(1024)}, f32[6912]{0:T(1024)}, /*index=5*/f32[16,961]{1,0:T(8,128)}), (f32[2304]{0:T(1024)}, f32[1152]{0:T(1024)}, f32[4608]{0:T(1024)}, ...) | async-done | bytes 126032 | tf_op jit(solution)/shard_map/psum | solution.py:318
  (512 shorter events, 283.5 us)
Async XLA Ops:
  7.2 272.5 %all-gather.8.cloned.1.call-start = ((), (), s32[]{:S(2)}) async-start(), calls=%async_computation.1 | async-start | bytes 17915904 | tf_op jit(solution)/shard_map/all_gather | solution.py:171
  7.9 338.8 %all-gather.10.cloned.1.call-start = ((), (), s32[]{:S(2)}) async-start(), calls=%async_computation.2 | async-start | bytes 8957952 | tf_op jit(solution)/shard_map/all_gather | solution.py:205
  8.7 395.3 %all-gather.12.cloned.1.call-start = ((), (), s32[]{:S(2)}) async-start(), calls=%async_computation.3 | async-start | bytes 2985984 | tf_op jit(solution)/shard_map/all_gather | solution.py:217
  9.4 545.9 %all-gather.14.cloned.1.call-start = ((), (), s32[]{:S(2)}) async-start(), calls=%async_computation.4 | async-start | bytes 11943936 | tf_op jit(solution)/shard_map/all_gather | solution.py:223
  10.0 698.0 %all-gather.16.cloned.1.call-start = ((), (), s32[]{:S(2)}) async-start(), calls=%async_computation.5 | async-start | bytes 11943936 | tf_op jit(solution)/shard_map/all_gather | solution.py:227
  10.6 1722.4 %reduce-scatter.4.cloned.1.call-start = ((), (), s32[]{:S(2)}) async-start(), calls=%async_computation.6 | async-start | bytes 53747712 | tf_op jit(solution)/shard_map/reduce_scatter | solution.py:305
  17.2 253.4 %copy-start.135 = (s32[2,256]{1,0:T(2,128)}, s32[2,256]{1,0:T(2,128)S(1)}, u32[]{:S(2)}) copy-start(s32[2,256]{1,0:T(2,128)S(1)} %get-tuple-element.193) | copy-start | bytes 6148
  17.2 370.5 %copy-start.98 = (s32[2,256]{1,0:T(2,128)}, s32[2,256]{1,0:T(2,128)S(1)}, u32[]{:S(2)}) copy-start(s32[2,256]{1,0:T(2,128)S(1)} %get-tuple-element.192) | copy-start | bytes 6148
  292.3 64.0 %copy-start.63 = (bf16[512,1152]{1,0:T(8,128)(2,1)}, bf16[512,1152]{1,0:T(8,128)(2,1)S(1)}, u32[]{:S(2)}) copy-start(bf16[512,1152]{1,0:T(8,128)(2,1)S(1)} %fusion.98) | copy-start | bytes 3538948
  398.8 12.0 copy-start.54
  461.2 309.8 %copy-start.74 = (f32[2,1152]{1,0:T(2,128)}, f32[2,1152]{1,0:T(2,128)S(1)}, u32[]{:S(2)}) copy-start(f32[2,1152]{1,0:T(2,128)S(1)} %get-tuple-element.239) | copy-start | bytes 27652
  464.0 321.5 %copy-start.81 = (f32[2,1152]{1,0:T(2,128)}, f32[2,1152]{1,0:T(2,128)S(1)}, u32[]{:S(2)}) copy-start(f32[2,1152]{1,0:T(2,128)S(1)} %get-tuple-element.235) | copy-start | bytes 27652
  555.3 11.7 copy-start.66
  555.3 11.7 copy-start.155
  708.0 11.6 copy-start.104
  757.2 13.2 copy-start.110
  757.2 13.8 copy-start.88
  757.2 13.8 copy-start.108
  757.2 13.8 copy-start.149
  771.0 14.5 copy-start.10
  771.0 14.5 copy-start.11
  771.0 14.5 copy-start.106
  771.0 14.5 copy-start.147
  785.5 14.2 copy-start.71
  931.0 17.3 copy-start.52
  948.3 16.7 copy-start.75
  948.3 16.7 copy-start.126
  948.3 16.7 copy-start.134
  984.2 815.0 %copy-start.154 = (u32[32]{0:T(128)S(1)}, u32[32]{0:T(128)}, u32[]{:S(2)}) copy-start(u32[32]{0:T(128)} %constant.195) | copy-start | bytes 388
  984.2 932.1 %all-gather.18.cloned.1.call-start = ((), (), s32[]{:S(2)}) async-start(), calls=%async_computation.7 | async-start | bytes 8294400 | tf_op jit(solution)/shard_map/all_gather | solution.py:309
  1797.0 3.4 collective-permute-start
  1820.5 232.0 %all-reduce.5.cloned.1.call-start = ((), (), s32[]{:S(2)}) async-start(), calls=%async_computation.8 | async-start | bytes 286720 | tf_op jit(solution)/shard_map/psum | solution.py:318
  (139 other events, 612.5 us)
Sparse Core Ops, SparseCore 0:
  10.2 216.5 all-gather.7
  228.9 117.7 all-gather.9
  348.9 55.0 all-gather.11
  406.0 149.1 all-gather.13
  557.3 150.6 all-gather.15
  984.3 748.6 reduce-scatter.3
  1820.6 57.1 all-gather.17
  1916.3 136.0 all-reduce.4
where the time goes:
time: 2070 us
  waiting for transfers between devices  1140 us (55%)
  local copies, waits for them, and re-layouts  442 us (21%)
  matrix products  327 us (16%)
  other arithmetic  72.9 us (4%)
  blocking collectives  62 us (3%)
    reduce_scatter x1, waiting for transfers between devices, local(): lax.psum_scatter(jnp.concatenate(pieces, axis=1).astype(jnp.bfloat16), 's...  749 us
    gather x2, local copies, waits for them, and re-layouts, local(): jnp.take(relative_table, relative_index(jnp.arange(GRID)), axis=1)  244 us
    all_gather x1, waiting for transfers between devices, local(): lax.all_gather(down_weight, 'seq', axis=0, tiled=True)  132 us
    psum x1, waiting for transfers between devices, local(): lax.psum((heads_part, merge_part, up_part, down_part, modulate_part, tabl...  114 us
    dot_general x9, matrix products, fold_rows(): return jnp.dot(left, portion, preferred_element_type=jnp.float32)  96.1 us
    all_gather x1, waiting for transfers between devices, local(): lax.all_gather(up_weight, 'seq', axis=0, tiled=True)  87.5 us
    dot_general x8, matrix products, right_transposed(): lax.dot_general(left, portion, (((1,), (1,)), ((), ())), preferred_elemen...  77.3 us
    unnamed x359, local copies, waits for them, and re-layouts  65.2 us
  transfers between devices with their start and end apart: 9, of which 6 were waited for; matrix products, arithmetic and copies ran while one was open for 25% of the time, Pallas kernels for 0%

commit v1 on v0

--- a/solution.py
+++ b/solution.py
@@ -14,6 +14,18 @@
 SAMP_DEV = 4
 GRID = 256
 epsilon = 1e-06
+
+
+def doubled_up(value, axis, dim):
+    ways, here = (lax.axis_size(axis), lax.axis_index(axis))
+    grown, reach = (value, 1)
+    while reach < ways:
+        theirs = lax.ppermute(grown, axis, [(d, d ^ reach) for d in range(ways)])
+        mine_first = jnp.concatenate([grown, theirs], axis=dim)
+        theirs_first = jnp.concatenate([theirs, grown], axis=dim)
+        grown = jnp.where(here & reach == 0, mine_first, theirs_first)
+        reach = 2 * reach
+    return grown
 
 
 def layer_norm(values):
@@ -219,9 +231,9 @@
         branch = branch.reshape(samples, GRID, D)
         middle = slab + gate_one * branch
         hidden_two = modulated(middle, scale_two, shift_two).astype(jnp.bfloat16).reshape(rows, D)
-        up_value = fold_rows(
-            hidden_two, lax.all_gather(up_weight, "seq", axis=0, tiled=True)
-        ) + up_bias.astype(jnp.float32)
+        up_value = fold_rows(hidden_two, doubled_up(up_weight, "seq", 0)) + up_bias.astype(
+            jnp.float32
+        )
         activated = gelu_tanh(up_value).astype(jnp.bfloat16)
         mlp_out = right_transposed(
             activated, lax.all_gather(down_weight, "seq", axis=0, tiled=True)

time: 2070 us -> 2320 us (1.12)
  waiting for transfers between devices: 1140 us -> 1360 us
    all_gather x1, waiting for transfers between devices: 54.5 us -> 183 us  [local(): lax.all_gather(heads_weight, 'seq', axis=0, tiled=True)]
    all_gather x1, waiting for transfers between devices: 4.54 us -> 87.6 us  [local(): lax.all_gather(merge_weight, 'seq', axis=0, tiled=True)]
    ppermute x0 -> x3, waiting for transfers between devices: none -> 45.3 us  [doubled_up(): theirs = lax.ppermute(grown, axis, [(d, d ^ reach) for d in range(ways)])]
    all_gather x1, waiting for transfers between devices: 132 us -> 90.1 us  [local(): lax.all_gather(down_weight, 'seq', axis=0, tiled=True)]
    unnamed x359 -> x419, local copies, waits for them, and re-layouts: 65.2 us -> 62.6 us
  transfers between devices with their start and end apart: 9 -> 12, of which waited for: 6 -> 7; matrix products, arithmetic and copies ran while one was open for 25% -> 24% of each run, Pallas kernels for 0% -> 0%
where the time goes in v1:
time: 2320 us; the launch traced here: 2310 us
  waiting for transfers between devices  1360 us (59%)
  local copies, waits for them, and re-layouts  440 us (19%)
  matrix products  336 us (14%)
  other arithmetic  87.1 us (4%)
  blocking collectives  62 us (3%)
    reduce_scatter x1, waiting for transfers between devices, local(): lax.psum_scatter(jnp.concatenate(pieces, axis=1).astype(jnp.bfloat16), 's...  749 us
    gather x2, local copies, waits for them, and re-layouts, local(): jnp.take(relative_table, relative_index(jnp.arange(GRID)), axis=1)  246 us
    all_gather x1, waiting for transfers between devices, local(): lax.all_gather(heads_weight, 'seq', axis=0, tiled=True)  183 us
    psum x1, waiting for transfers between devices, local(): lax.psum((heads_part, merge_part, up_part, down_part, modulate_part, tabl...  111 us
    dot_general x9, matrix products, fold_rows(): return jnp.dot(left, portion, preferred_element_type=jnp.float32)  101 us
    all_gather x1, waiting for transfers between devices, local(): lax.all_gather(up_weight, 'seq', axis=0, tiled=True)  90.5 us
    all_gather x1, waiting for transfers between devices, local(): lax.all_gather(down_weight, 'seq', axis=0, tiled=True)  90.1 us
    all_gather x1, waiting for transfers between devices, local(): lax.all_gather(merge_weight, 'seq', axis=0, tiled=True)  87.6 us
  transfers between devices with their start and end apart: 12, of which 7 were waited for; matrix products, arithmetic and copies ran while one was open for 24% of the time, Pallas kernels for 0%

profile of v1, /device:TPU:8, one launch (start us, length us, event | category | flops | bytes accessed | tf_op | source)
XLA Modules:
  0.0 2308.6 jit_solution(9363438159363770707)
XLA Ops:
  14.6 45.3 %collective-permute-done = bf16[144,4608]{1,0:T(8,128)(2,1)} collective-permute-done((bf16[144,4608]{1,0:T(8,128)(2,1)}, bf16[144,4608]{1,0:T(8,128)(2,1)}, u32[]{:S(2)}, u32[]{:S(2)}) %collective-permute-start) | collective-permute-done | bytes 1327136 | tf_op jit(solution)/shard_map/ppermute | solution.py:23
  66.5 228.9 %gather_fusion = bf16[65536,16]{1,0:T(8,128)(2,1)} fusion(bf16[16,961]{0,1:T(8,128)(2,1)S(1)} %copy.147, s32[65536]{0:T(1024)S(1)} %broadcast_clamp_fusion), kind=kCustom, calls=%fused_computation | custom fusion | bytes 4456448 | tf_op jit(solution)/shard_map/jit(_take)/gather | solution.py:180
  295.4 16.8 copy.148
  352.5 182.5 %all-gather.10.cloned.1.call-done = bf16[1152,3456]{1,0:T(8,128)(2,1)} async-done(((bf16[144,3456]{1,0:T(8,128)(2,1)}), bf16[1152,3456]{1,0:T(8,128)(2,1)}) %all-gather.10.cloned.1.call-update) | async-done | bytes 7962640 | tf_op jit(solution)/shard_map/all_gather | solution.py:217
  535.0 9.5 add_convert_fusion.1
  550.4 8.5 reshape.859
  576.6 87.6 %all-gather.12.cloned.1.call-done = bf16[1152,1152]{1,0:T(8,128)(2,1)} async-done(((bf16[144,1152]{1,0:T(8,128)(2,1)}), bf16[1152,1152]{1,0:T(8,128)(2,1)}) %all-gather.12.cloned.1.call-update) | async-done | bytes 2654224 | tf_op jit(solution)/shard_map/all_gather | solution.py:229
  672.1 10.9 add_convert_fusion
  688.8 8.3 reshape.861
  725.3 90.1 %all-gather.14.cloned.1.call-done = bf16[1152,4608]{1,0:T(8,128)(2,1)} async-done(((bf16[144,4608]{1,0:T(8,128)(2,1)}), bf16[1152,4608]{1,0:T(8,128)(2,1)}) %all-gather.14.cloned.1.call-update) | async-done | bytes 10616848 | tf_op jit(solution)/shard_map/all_gather | solution.py:239
  815.4 11.7 fusion.234
  827.1 8.8 fusion.235
  835.9 13.5 fusion.105
  849.3 28.3 %fusion.11 = (bf16[512,4608]{1,0:T(8,128)(2,1)}, bf16[512,4608]{1,0:T(8,128)(2,1)}, bf16[512,4608]{1,0:T(8,128)(2,1)}, bf16[512,4608]{1,0:T(8,128)(2,1)}) fusion(f32[512,4608]{1,0:T(8,128)} %fusion.234, f32[4608]{0:T(1024)} %convert_element_type.243, f32[512,4608]{1,0:T(8,128)} %fusion.105, f32[512,4608]{1,0:T(8,128)} %fusion.235, ...), kind=kOutput, calls=%fused_computation.22 | convolution fusion | flops 5592121344 | bytes 59000832 | tf_op jit(solution)/shard_map/dot_general | solution.py:46
  877.6 90.5 %all-gather.16.cloned.1.call-done = bf16[1152,4608]{1,0:T(8,128)(2,1)} async-done(((bf16[144,4608]{1,0:T(8,128)(2,1)}), bf16[1152,4608]{1,0:T(8,128)(2,1)}) %all-gather.16.cloned.1.call-update) | async-done | bytes 10616848 | tf_op jit(solution)/shard_map/all_gather | solution.py:256
  968.1 13.0 multiply_reduce_fusion.11
  981.7 15.0 fusion.214
  998.0 11.5 multiply_reduce_fusion.9
  1010.1 14.0 fusion.215
  1108.5 10.5 multiply_reduce_fusion.10
  1125.7 10.3 multiply_reduce_fusion.8
  1154.8 14.3 fusion.4
  1171.7 15.7 fusion.3
  1187.4 17.6 fusion.2
  1216.2 8.6 fusion.1
  1224.9 749.0 %reduce-scatter.4.cloned.1.call-done = bf16[144,20736]{1,0:T(8,128)(2,1)} async-done(((bf16[1152,20736]{1,0:T(8,128)(2,1)}), bf16[144,20736]{1,0:T(8,128)(2,1)}) %reduce-scatter.4.cloned.1.call-update) | async-done | bytes 5971984 | tf_op jit(solution)/shard_map/reduce_scatter | solution.py:317
  1973.8 62.0 %fusion = bf16[40,20736]{1,0:T(8,128)(2,1)} fusion(bf16[144,20736]{1,0:T(8,128)(2,1)} %reduce-scatter.4.cloned.1.call-done), kind=kCustom, calls=%all-reduce-scatter | all-reduce-scatter fusion | flops 3317761 | bytes 7631360
  2041.3 17.0 concatenate.102
  2076.5 19.5 add.547
  2096.0 33.3 %fusion.187 = f32[31,16,16,16,1]{0,3,2,4,1:T(8,128)} fusion(f32[16,16,16,16,16]{4,3,2,1,0:T(8,128)} %add.547, s32[16,16]{1,0:T(8,128)S(1)} %subtract_add_fusion), kind=kOutput, calls=%fused_computation.263 | convolution fusion | flops 390078208 | bytes 4703232 | tf_op jit(solution)/shard_map/hwxyz,wya->haxz/dot_general | solution.py:155
  2157.0 10.3 reshape.899
  2181.9 111.4 %all-reduce.5.cloned.1.call-done = (f32[2304]{0:T(1024)}, f32[1152]{0:T(1024)}, f32[4608]{0:T(1024)}, f32[1152]{0:T(1024)}, f32[6912]{0:T(1024)}, /*index=5*/f32[16,961]{1,0:T(8,128)}) async-done(((f32[2304]{0:T(1024)}, f32[1152]{0:T(1024)}, f32[4608]{0:T(1024)}, f32[1152]{0:T(1024)}, f32[6912]{0:T(1024)}, /*index=5*/f32[16,961]{1,0:T(8,128)}), (f32[2304]{0:T(1024)}, f32[1152]{0:T(1024)}, f32[4608]{0:T(1024)}, ...) | async-done | bytes 126032 | tf_op jit(solution)/shard_map/psum | solution.py:330
  (581 shorter events, 317.3 us)
Async XLA Ops:
  7.2 333.5 %all-gather.8.cloned.1.call-start = ((), (), s32[]{:S(2)}) async-start(), calls=%async_computation.1 | async-start | bytes 17915904 | tf_op jit(solution)/shard_map/all_gather | solution.py:183
  7.9 527.1 %all-gather.10.cloned.1.call-start = ((), (), s32[]{:S(2)}) async-start(), calls=%async_computation.2 | async-start | bytes 8957952 | tf_op jit(solution)/shard_map/all_gather | solution.py:217
  8.7 655.5 %all-gather.12.cloned.1.call-start = ((), (), s32[]{:S(2)}) async-start(), calls=%async_computation.3 | async-start | bytes 2985984 | tf_op jit(solution)/shard_map/all_gather | solution.py:229
  9.4 806.0 %all-gather.14.cloned.1.call-start = ((), (), s32[]{:S(2)}) async-start(), calls=%async_computation.4 | async-start | bytes 11943936 | tf_op jit(solution)/shard_map/all_gather | solution.py:239
  10.0 958.1 %all-gather.16.cloned.1.call-start = ((), (), s32[]{:S(2)}) async-start(), calls=%async_computation.5 | async-start | bytes 11943936 | tf_op jit(solution)/shard_map/all_gather | solution.py:256
  10.0 49.9 %collective-permute-start = (bf16[144,4608]{1,0:T(8,128)(2,1)}, bf16[144,4608]{1,0:T(8,128)(2,1)}, u32[]{:S(2)}, u32[]{:S(2)}) collective-permute-start(bf16[144,4608]{1,0:T(8,128)(2,1)} %param.24), channel_id=1, source_target_pairs={{0,1},{1,0},{2,3},{3,2},{4,5},{5,4},{6,7},{7,6},{8,9},{9,8},{10,11... | collective-permute-start | bytes 3981320 | tf_op jit(solution)/shard_map/ppermute | solution.py:23
  11.6 1962.2 %reduce-scatter.4.cloned.1.call-start = ((), (), s32[]{:S(2)}) async-start(), calls=%async_computation.6 | async-start | bytes 53747712 | tf_op jit(solution)/shard_map/reduce_scatter | solution.py:317
  12.1 53.0 %copy-start.115 = (f32[512]{0:T(512)}, f32[512]{0:T(512)S(1)}, u32[]{:S(2)}) copy-start(f32[512]{0:T(512)S(1)} %get-tuple-element.237) | copy-start | bytes 6148
  12.1 53.5 %copy-start.116 = (f32[512]{0:T(512)}, f32[512]{0:T(512)S(1)}, u32[]{:S(2)}) copy-start(f32[512]{0:T(512)S(1)} %get-tuple-element.236) | copy-start | bytes 6148
  14.5 298.3 %copy-start.150 = (pred[2,256]{1,0:T(4,128)(4,1)}, pred[2,256]{1,0:T(4,128)(4,1)S(1)}, u32[]{:S(2)}) copy-start(pred[2,256]{1,0:T(4,128)(4,1)S(1)} %get-tuple-element.239) | copy-start | bytes 1540
  14.5 298.8 %copy-start.157 = (pred[2,256]{1,0:T(4,128)(4,1)}, pred[2,256]{1,0:T(4,128)(4,1)S(1)}, u32[]{:S(2)}) copy-start(pred[2,256]{1,0:T(4,128)(4,1)S(1)} %get-tuple-element.238) | copy-start | bytes 1540
  14.6 51.7 %copy-start.154 = (bf16[6912]{0:T(1024)(128)(2,1)S(1)}, bf16[6912]{0:T(1024)(128)(2,1)}, u32[]{:S(2)}) copy-start(bf16[6912]{0:T(1024)(128)(2,1)} %param.29) | copy-start | bytes 41476
  14.6 51.7 %copy-start.114 = (bf16[16,961]{1,0:T(8,128)(2,1)S(1)}, bf16[16,961]{1,0:T(8,128)(2,1)}, u32[]{:S(2)}) copy-start(bf16[16,961]{1,0:T(8,128)(2,1)} %param.30) | copy-start | bytes 92260
  63.9 266.5 %collective-permute-start.1 = (bf16[288,4608]{1,0:T(8,128)(2,1)}, bf16[288,4608]{1,0:T(8,128)(2,1)}, u32[]{:S(2)}, u32[]{:S(2)}) collective-permute-start(bf16[288,4608]{1,0:T(8,128)(2,1)} %maximum_select_fusion.2), channel_id=1, source_target_pairs={{0,2},{1,3},{2,0},{3,1},{4,6},{5,7},{6,4},{7,5},{8,10},{9,11},{10,... | collective-permute-start | bytes 7962632 | tf_op jit(solution)/shard_map/ppermute | solution.py:23
  295.4 18.6 copy-start.156
  295.4 19.2 copy-start.179
  295.4 20.9 copy-start.180
  316.3 247.9 %copy-start.112 = (s32[2,256]{1,0:T(2,128)}, s32[2,256]{1,0:T(2,128)S(1)}, u32[]{:S(2)}) copy-start(s32[2,256]{1,0:T(2,128)S(1)} %get-tuple-element.192) | copy-start | bytes 6148
  338.1 497.7 %collective-permute-start.2 = (bf16[576,4608]{1,0:T(8,128)(2,1)}, bf16[576,4608]{1,0:T(8,128)(2,1)}, u32[]{:S(2)}, u32[]{:S(2)}) collective-permute-start(bf16[576,4608]{1,0:T(8,128)(2,1)} %maximum_select_fusion.1), channel_id=1, source_target_pairs={{0,4},{1,5},{2,6},{3,7},{4,0},{5,1},{6,2},{7,3},{8,12},{9,13},{10,... | collective-permute-start | bytes 15925256 | tf_op jit(solution)/shard_map/ppermute | solution.py:23
  352.5 192.1 %copy-start.67 = (bf16[512,1152]{1,0:T(8,128)(2,1)}, bf16[512,1152]{1,0:T(8,128)(2,1)S(1)}, u32[]{:S(2)}) copy-start(bf16[512,1152]{1,0:T(8,128)(2,1)S(1)} %fusion.98) | copy-start | bytes 3538948
  573.8 90.3 %copy-start.117 = (f32[512]{0:T(512)S(1)}, f32[512]{0:T(512)}, u32[]{:S(2)}) copy-start(f32[512]{0:T(512)} %copy-done.116) | copy-start | bytes 6148
  575.3 95.8 %copy-start.57 = (bf16[144,8,2,256]{3,1,2,0:T(8,128)(2,1)}, bf16[144,8,2,256]{3,1,2,0:T(8,128)(2,1)S(1)}, u32[]{:S(2)}) copy-start(bf16[144,8,2,256]{3,1,2,0:T(8,128)(2,1)S(1)} %copy.251) | copy-start | bytes 3538948
  1150.5 20.4 slice-start.4
  1187.3 17.7 copy-start.82
  1187.4 17.7 copy-start.137
  1187.4 17.7 copy-start.149
  1187.4 17.7 copy-start.152
  1187.4 17.7 copy-start.161
  1224.8 815.2 %copy-start.182 = (u32[32]{0:T(128)S(1)}, u32[32]{0:T(128)}, u32[]{:S(2)}) copy-start(u32[32]{0:T(128)} %constant.198) | copy-start | bytes 388
  1224.8 932.2 %all-gather.18.cloned.1.call-start = ((), (), s32[]{:S(2)}) async-start(), calls=%async_computation.7 | async-start | bytes 8294400 | tf_op jit(solution)/shard_map/all_gather | solution.py:321
  2037.9 3.4 collective-permute-start.3
  2061.4 231.9 %all-reduce.5.cloned.1.call-start = ((), (), s32[]{:S(2)}) async-start(), calls=%async_computation.8 | async-start | bytes 286720 | tf_op jit(solution)/shard_map/psum | solution.py:330
  (171 other events, 985.6 us)
Sparse Core Ops, SparseCore 0:
  10.2 265.4 all-gather.7
  277.9 257.1 all-gather.9
  537.2 126.8 all-gather.11
  666.2 149.1 all-gather.13
  817.4 150.6 all-gather.15
  1224.9 748.8 reduce-scatter.3
  2061.5 57.1 all-gather.17
  2157.1 136.1 all-reduce.4
